TPU v7x, 32 devices: a whole 2x2x4 slice. The times are simulated.
32 devices in a mesh: dp: 8 (over y, x, core), tensor: 4 (over z).
Axes of the slice: x: 2, y: 2, z: 4, core: 2. Of those that a mesh axis runs over, the one named last changes fastest.
Arguments:
- hidden_in: bfloat16 [32, 512, 768], P('dp'), may hold values from -6 to 6
- out_grad: bfloat16 [32, 512, 768], P('dp'), may hold values from -3 to 3
- segment_ids: int32 [32, 512], P('dp'), may hold values from 0 to 7, never falling along the last dimension, each value on 1 to 256 neighbouring positions
- step_count: int32 [1], replicated, may hold values from 1 to 199999
- qkv_state: float32 [3, 768, 3, 768], P(None, 'dp', None, 'tensor'), as said below
- qv_bias_state: float32 [3, 2, 12, 64], P(None, None, 'tensor', 'dp'), as said below
- out_state: float32 [3, 768, 768], P(None, 'tensor', 'dp'), as said below
- up_state: float32 [3, 768, 3072], P(None, 'dp', 'tensor'), as said below
- up_bias_state: float32 [3, 24, 128], P(None, 'tensor', 'dp'), as said below
- down_state: float32 [3, 3072, 768], P(None, 'tensor', 'dp'), as said below
- vector_state: float32 [3, 6, 768], P(None, None, 'dp'), as said below
Outputs:
- hidden_out: bfloat16 [32, 512, 768], P('dp')
- grad_in: bfloat16 [32, 512, 768], P('dp')
- grad_qkv: float32 [768, 3, 768], P('dp', None, 'tensor')
- grad_qv_bias: float32 [2, 12, 64], P(None, 'tensor', 'dp')
- grad_out: float32 [768, 768], P('tensor', 'dp')
- grad_up: float32 [768, 3072], P('dp', 'tensor')
- grad_up_bias: float32 [24, 128], P('tensor', 'dp')
- grad_down: float32 [3072, 768], P('tensor', 'dp')
- grad_vectors: float32 [6, 768], P(None, 'dp')
- new_qkv_state: float32 [2, 768, 3, 768], P(None, 'dp', None, 'tensor')
- new_qv_bias_state: float32 [2, 2, 12, 64], P(None, None, 'tensor', 'dp')
- new_out_state: float32 [2, 768, 768], P(None, 'tensor', 'dp')
- new_up_state: float32 [2, 768, 3072], P(None, 'dp', 'tensor')
- new_up_bias_state: float32 [2, 24, 128], P(None, 'tensor', 'dp')
- new_down_state: float32 [2, 3072, 768], P(None, 'tensor', 'dp')
- new_vector_state: float32 [2, 6, 768], P(None, None, 'dp')
- plan: float32 [3], replicated
Inputs may be any that keep to these rules, and one draw needn't show every extreme that they name: `segment_ids`: within each packed row the fragment numbers never fall; a token attends exactly to the tokens of its own row with the same number. `qkv_state`: index 2 (second moments) is positive. `qv_bias_state`: index 2 (second moments) is positive. `out_state`: index 2 (second moments) is positive. `up_state`: index 2 (second moments) is positive. `up_bias_state`: index 2 (second moments) is positive. `down_state`: index 2 (second moments) is positive. `vector_state`: index 2 (second moments) is positive.
All inputs are finite; a program needn't handle non-finite values.
Results may differ from a plain program's by a relative error of at most 0.023.
The roundings to bfloat16 on the way count: a program that leaves them out, or rounds other values in their place, can miss the bound.
Values may be sent and summed in bfloat16 or wider, within the bound.
No kernel may reach another device: no remote copies, remote signals or barrier semaphores. Data moves between devices by JAX's collectives and lax.ppermute only.
A program may use at most 192 MiB of HBM per device.

v0:
```python
import math
import jax
import jax.numpy as jnp
from jax import lax
from jax.sharding import PartitionSpec as P

HD = 64
norm_eps = 1e-05
beta_first = 0.9
beta_second = 0.999
warm_steps = 10000.0
total_steps = 200000.0


def layer_norm(value, gain, shift):
    center = value - jnp.mean(value, axis=-1, keepdims=True)
    spread = jnp.mean(center * center, axis=-1, keepdims=True)
    return center * lax.rsqrt(spread + norm_eps) * gain + shift


def gelu_exact(value):
    return 0.5 * value * (1.0 + lax.erf(value * 0.7071067811865476))


def scores_of(query, key_rows, segments):
    raw = jnp.einsum(
        "bqhd,bkhd->bhqk", query, key_rows, preferred_element_type=jnp.float32
    ) * HD ** (-0.5)
    same = segments[:, :, None] == segments[:, None, :]
    return jnp.where(same[:, None], raw, -1e30)


def contract_rows(left, right):
    return lax.dot_general(
        left, right, (((0,), (0,)), ((), ())), preferred_element_type=jnp.float32
    )


def contract_cols(left, right):
    return lax.dot_general(
        left, right, (((1,), (1,)), ((), ())), preferred_element_type=jnp.float32
    )


def moment_update(state, grad):
    moment_one = beta_first * state[1] + (1.0 - beta_first) * grad
    moment_two = beta_second * state[2] + (1.0 - beta_second) * grad * grad
    return jnp.stack([moment_one, moment_two])


def body(
    hidden_in,
    out_grad,
    segment_ids,
    step_count,
    qkv_state,
    qv_bias_state,
    out_state,
    up_state,
    up_bias_state,
    down_state,
    vector_state,
):
    bf = jnp.bfloat16
    fl = jnp.float32
    w_qkv, b_qv, w_out, w_up, b_up, w_down, vectors = (
        lax.all_gather(qkv_state[0].astype(bf), "dp", axis=0, tiled=True),
        lax.all_gather(qv_bias_state[0].astype(bf), "dp", axis=2, tiled=True),
        lax.all_gather(out_state[0].astype(bf), "dp", axis=1, tiled=True),
        lax.all_gather(up_state[0].astype(bf), "dp", axis=0, tiled=True),
        lax.all_gather(up_bias_state[0].astype(bf), "dp", axis=1, tiled=True),
        lax.all_gather(down_state[0].astype(bf), "dp", axis=1, tiled=True),
        lax.all_gather(vector_state[0].astype(bf), "dp", axis=1, tiled=True),
    )
    count, length, width_model = hidden_in.shape
    rows = count * length
    heads_local = b_qv.shape[1]
    head_width = heads_local * HD
    ff_local = w_up.shape[1]
    scale = HD ** (-0.5)
    plain = hidden_in.reshape(rows, width_model)
    cotangent = out_grad.reshape(rows, width_model)
    vec = vectors.astype(fl)
    proj = jnp.einsum("td,dcf->tcf", plain, w_qkv, preferred_element_type=fl)
    bias_f = b_qv.astype(fl).reshape(2, head_width)
    bias = jnp.stack([bias_f[0], jnp.zeros((head_width,), fl), bias_f[1]])
    proj_b = (proj + bias[None]).astype(bf)
    heads = proj_b.reshape(count, length, 3, heads_local, HD)
    query = heads[:, :, 0]
    key_rows = heads[:, :, 1]
    value_rows = heads[:, :, 2]
    scores = scores_of(query, key_rows, segment_ids)
    top = jnp.max(scores, axis=-1, keepdims=True)
    expd = jnp.exp(scores - top)
    denom = jnp.sum(expd, axis=-1, keepdims=True)
    log_total = top + jnp.log(denom)
    probs_b = (expd / denom).astype(bf)
    context = (
        jnp.einsum("bhqk,bkhd->bqhd", probs_b, value_rows, preferred_element_type=fl)
        .astype(bf)
        .reshape(rows, head_width)
    )
    attn_part = jnp.dot(context, w_out, preferred_element_type=fl)
    attn = lax.psum(attn_part.astype(jnp.bfloat16), "tensor").astype(jnp.float32)
    first, first_pull = jax.vjp(layer_norm, plain.astype(fl) + attn + vec[4], vec[0], vec[1])
    first_b = first.astype(bf)
    up = jnp.dot(first_b, w_up, preferred_element_type=fl) + b_up.astype(fl).reshape(ff_local)
    act, gelu_pull = jax.vjp(gelu_exact, up)
    act_b = act.astype(bf)
    ffn_part = jnp.dot(act_b, w_down, preferred_element_type=fl)
    ffn = lax.psum(ffn_part.astype(jnp.bfloat16), "tensor").astype(jnp.float32)
    out, second_pull = jax.vjp(layer_norm, first + ffn + vec[5], vec[2], vec[3])
    grad_r2, grad_g2, grad_b2 = second_pull(cotangent.astype(fl))
    grad_ffn = grad_r2.astype(bf)
    grad_down = contract_rows(act_b, grad_ffn)
    grad_act = contract_cols(grad_ffn, w_down)
    grad_up_b = gelu_pull(grad_act)[0].astype(bf)
    grad_wup = contract_rows(first_b, grad_up_b)
    grad_bup = jnp.sum(grad_up_b, axis=0, dtype=fl).reshape(b_up.shape)
    feed_part = contract_cols(grad_up_b, w_up)
    feed_back = lax.psum(feed_part.astype(jnp.bfloat16), "tensor").astype(jnp.float32)
    grad_first = grad_r2 + feed_back.astype(bf).astype(fl)
    grad_r1, grad_g1, grad_b1 = first_pull(grad_first)
    grad_attn = grad_r1.astype(bf)
    grad_wout = contract_rows(context, grad_attn)
    grad_context = (
        contract_cols(grad_attn, w_out).astype(bf).reshape(count, length, heads_local, HD)
    )
    again = scores_of(query, key_rows, segment_ids)
    probs = jnp.exp(again - log_total)
    probs_again = probs.astype(bf)
    grad_probs = jnp.einsum("bqhd,bkhd->bhqk", grad_context, value_rows, preferred_element_type=fl)
    grad_value = jnp.einsum("bhqk,bqhd->bkhd", probs_again, grad_context, preferred_element_type=fl)
    row_dot = jnp.sum(probs * grad_probs, axis=-1, keepdims=True)
    grad_scores = (probs * (grad_probs - row_dot)).astype(bf)
    grad_query = (
        jnp.einsum("bhqk,bkhd->bqhd", grad_scores, key_rows, preferred_element_type=fl) * scale
    )
    grad_key = jnp.einsum("bhqk,bqhd->bkhd", grad_scores, query, preferred_element_type=fl) * scale
    grad_proj = (
        jnp.stack([grad_query, grad_key, grad_value], axis=2)
        .astype(bf)
        .reshape(rows, 3, head_width)
    )
    proj_sums = jnp.sum(grad_proj, axis=0, dtype=fl)
    grad_bqv = jnp.stack([proj_sums[0], proj_sums[2]]).reshape(2, heads_local, HD)
    grad_wqkv = jnp.einsum("td,tcf->dcf", plain, grad_proj, preferred_element_type=fl)
    input_part = jnp.einsum("tcf,dcf->td", grad_proj, w_qkv, preferred_element_type=fl)
    vec_part = jnp.stack(
        [grad_g1, grad_b1, grad_g2, grad_b2, jnp.sum(grad_r1, axis=0), jnp.sum(grad_r2, axis=0)]
    )
    input_back = lax.psum(input_part.astype(jnp.bfloat16), "tensor").astype(jnp.float32)
    grad_in = (grad_r1 + input_back.astype(bf).astype(fl)).astype(bf).reshape(hidden_in.shape)
    hidden_out = out.astype(bf).reshape(hidden_in.shape)
    summed = (
        lax.psum_scatter(grad_wqkv, "dp", scatter_dimension=0, tiled=True),
        lax.psum_scatter(grad_bqv, "dp", scatter_dimension=2, tiled=True),
        lax.psum_scatter(grad_wout, "dp", scatter_dimension=1, tiled=True),
        lax.psum_scatter(grad_wup, "dp", scatter_dimension=0, tiled=True),
        lax.psum_scatter(grad_bup, "dp", scatter_dimension=1, tiled=True),
        lax.psum_scatter(grad_down, "dp", scatter_dimension=1, tiled=True),
        lax.psum_scatter(vec_part, "dp", scatter_dimension=1, tiled=True),
    )
    steps_f = step_count[0].astype(fl)
    factor = jnp.minimum(steps_f / warm_steps, (total_steps - steps_f) / (total_steps - warm_steps))
    fix_first = 1.0 - jnp.exp(steps_f * math.log(beta_first))
    fix_second = 1.0 - jnp.exp(steps_f * math.log(beta_second))
    states = (
        qkv_state,
        qv_bias_state,
        out_state,
        up_state,
        up_bias_state,
        down_state,
        vector_state,
    )
    news = tuple((moment_update(s, g) for s, g in zip(states, summed)))
    plan = jnp.stack([factor, fix_first, fix_second])
    return (
        hidden_out,
        grad_in,
        summed[0],
        summed[1],
        summed[2],
        summed[3],
        summed[4],
        summed[5],
        summed[6],
        news[0],
        news[1],
        news[2],
        news[3],
        news[4],
        news[5],
        news[6],
        plan,
    )


def solution(mesh):
    return jax.shard_map(
        body,
        mesh=mesh,
        in_specs=(
            P("dp", None, None),
            P("dp", None, None),
            P("dp", None),
            P(),
            P(None, "dp", None, "tensor"),
            P(None, None, "tensor", "dp"),
            P(None, "tensor", "dp"),
            P(None, "dp", "tensor"),
            P(None, "tensor", "dp"),
            P(None, "tensor", "dp"),
            P(None, None, "dp"),
        ),
        out_specs=(
            P("dp", None, None),
            P("dp", None, None),
            P("dp", None, "tensor"),
            P(None, "tensor", "dp"),
            P("tensor", "dp"),
            P("dp", "tensor"),
            P("tensor", "dp"),
            P("tensor", "dp"),
            P(None, "dp"),
            P(None, "dp", None, "tensor"),
            P(None, None, "tensor", "dp"),
            P(None, "tensor", "dp"),
            P(None, "dp", "tensor"),
            P(None, "tensor", "dp"),
            P(None, "tensor", "dp"),
            P(None, None, "dp"),
            P(),
        ),
        check_vma=False,
    )
```

profile of v0, /device:TPU:0, one launch (start us, length us, event | category | flops | bytes accessed | tf_op | source)
XLA Modules:
  0.0 760.8 jit_solution(6386560561636301362)
XLA Ops:
  9.0 10.6 %all-gather.1 = bf16[1,2,3,64]{2,1,0,3:T(2,128)(2,1)S(1)} all-gather(bf16[1,2,3,8]{2,1,0,3:T(2,128)(2,1)S(1)} %copy.181), channel_id=3, replica_groups=mesh['dp'=8,'tensor'=4] {'dp'}, dimensions={3}, use_global_device_ids=true | all-gather | bytes 864 | tf_op jit(solution)/shard_map/all_gather | solution.py:68
  22.8 11.3 %all-gather.2 = bf16[1,192,768]{1,0,2:T(2,128)(2,1)} all-gather(bf16[1,192,96]{1,0,2:T(2,128)(2,1)S(1)} %copy.142), channel_id=4, replica_groups=mesh['dp'=8,'tensor'=4] {'dp'}, dimensions={2}, use_global_device_ids=true | all-gather | bytes 331776 | tf_op jit(solution)/shard_map/all_gather | solution.py:69
  34.1 2.2 copy.143
  36.3 2.3 broadcast_compare_fusion
  38.6 15.8 %all-gather = bf16[1,768,3,192]{3,2,0,1:T(4,128)(2,1)} all-gather(bf16[1,96,3,192]{3,2,0,1:T(4,128)(2,1)} %copy.132), channel_id=2, replica_groups=mesh['dp'=8,'tensor'=4] {'dp'}, dimensions={1}, use_global_device_ids=true | all-gather | bytes 995328 | tf_op jit(solution)/shard_map/all_gather | solution.py:67
  54.4 3.4 copy.133
  57.9 3.2 fusion.74
  61.2 1.7 add_convert_fusion.5
  62.9 6.2 reshape.215
  69.1 2.4 fusion.69
  71.5 4.4 fusion.73
  76.0 1.8 fusion
  77.8 2.8 copy-done
  80.7 2.3 fusion.22
  84.7 2.7 convolution_convert_fusion.2
  87.5 1.6 slice.205
  89.3 1.6 slice.204
  93.2 8.7 %all-gather.5 = bf16[1,6,128]{1,0,2:T(2,128)(2,1)S(1)} all-gather(bf16[1,6,16]{1,0,2:T(2,128)(2,1)} %copy.145), channel_id=7, replica_groups=mesh['dp'=8,'tensor'=4] {'dp'}, dimensions={2}, use_global_device_ids=true | all-gather | bytes 1728 | tf_op jit(solution)/shard_map/all_gather | solution.py:71
  103.2 10.8 %all-gather.3 = bf16[1,6,768]{1,0,2:T(2,128)(2,1)S(1)} all-gather(bf16[1,6,96]{1,0,2:T(2,128)(2,1)S(1)} %copy.185), channel_id=5, replica_groups=mesh['dp'=8,'tensor'=4] {'dp'}, dimensions={2}, use_global_device_ids=true | all-gather | bytes 10368 | tf_op jit(solution)/shard_map/all_gather | solution.py:73
  114.4 13.0 %slice_reduce_fusion.1 = (f32[768]{0:T(1024)S(1)}, f32[768]{0:T(1024)S(1)}, f32[768]{0:T(1024)S(1)}, f32[768]{0:T(1024)S(1)}, f32[768]{0:T(1024)S(1)}, /*index=5*/f32[768]{0:T(1024)S(1)}) fusion(f32[1,6,768]{1,0,2:T(1,128)S(1)} %convert_element_type.169), kind=kLoop, calls=%fused_computation.78 | loop fusion | bytes 36864 | tf_op jit(solution)/shard_map/slice | solution.py:112
  127.4 81.6 %all-reduce.6.cloned.1.call-done = bf16[2048,768]{1,0:T(8,128)(2,1)} async-done(((bf16[2048,768]{1,0:T(8,128)(2,1)}), bf16[2048,768]{1,0:T(8,128)(2,1)}) %all-reduce.6.cloned.1.call-update) | async-done | bytes 3145744 | tf_op jit(solution)/shard_map/psum | solution.py:104
  209.0 3.1 fusion.11
  212.1 3.7 multiply_reduce_fusion.4
  215.8 7.4 multiply_convert_fusion.1
  223.3 6.2 convolution_convert_fusion.1
  229.7 120.0 %all-reduce.8.cloned.1.call-done = bf16[2048,768]{1,0:T(8,128)(2,1)} async-done(((bf16[2048,768]{1,0:T(8,128)(2,1)}), bf16[2048,768]{1,0:T(8,128)(2,1)}) %all-reduce.8.cloned.1.call-update) | async-done | bytes 3145744 | tf_op jit(solution)/shard_map/psum | solution.py:111
  349.7 4.8 fusion.67
  356.4 3.0 fusion.7
  359.5 4.3 fusion.66
  363.8 5.9 convert_reduce_fusion.1
  369.7 1.7 copy-done.35
  371.5 4.0 convolution_convert_fusion
  376.4 8.0 %fusion.60 = f32[768,768]{0,1:T(8,128)} fusion(bf16[2048,768]{1,0:T(8,128)(2,1)} %copy-done.36, f32[2048,768]{1,0:T(8,128)} %copy-done.2, f32[2048]{0:T(1024)S(1)} %negate_multiply_fusion.1), kind=kOutput, calls=%fused_computation.147 | convolution fusion | flops 2419064832 | bytes 11804672 | tf_op jit(solution)/shard_map/dot_general | solution.py:34
  384.5 8.0 %fusion.61 = f32[768,768]{1,0:T(8,128)} fusion(bf16[2048,768]{1,0:T(8,128)(2,1)} %copy-done.35, f32[2048,768]{1,0:T(8,128)} %get-tuple-element.123, f32[768]{0:T(1024)} %copy-done.24, f32[768]{0:T(1024)} %copy-done.22, f32[2048]{0:T(1024)S(1)} %fusion.49), kind=kOutput, calls=%fused_computation.148 | convolution fusion | flops 2422210560 | bytes 11810816 | tf_op jit(solution)/shard_map/dot_general | solution.py:34
  392.8 102.9 %all-reduce.10.cloned.1.call-done = bf16[2048,768]{1,0:T(8,128)(2,1)} async-done(((bf16[2048,768]{1,0:T(8,128)(2,1)}), bf16[2048,768]{1,0:T(8,128)(2,1)}) %all-reduce.10.cloned.1.call-update) | async-done | bytes 3145744 | tf_op jit(solution)/shard_map/psum | solution.py:121
  495.7 8.0 %multiply_reduce_fusion.1 = (f32[768]{0:T(1024)}, f32[2048]{0:T(1024)S(1)}, f32[768]{0:T(1024)}, f32[768]{0:T(1024)}) fusion(f32[2048,768]{1,0:T(8,128)} %get-tuple-element.123, f32[2048]{0:T(1024)S(1)} %fusion.49, bf16[2048,768]{1,0:T(8,128)(2,1)} %all-reduce.10.cloned.1.call-done, f32[2048,768]{1,0:T(8,128)} %copy-done.2, ...), kind=kLoop, calls=%fused_computation.19 | loop fusion | flops 17297152 | bytes 15765504 | tf_op jit(solution)/shard_map/transpose(jvp())/reduce_sum | solution.py:18
  503.7 6.1 fusion.65
  509.8 2.6 copy-done.3
  512.4 2.2 convolution_convert_fusion.3
  514.7 3.0 reshape.218
  517.6 8.3 %multiply_reduce_fusion = (f32[4,3,512]{2,1,0:T(4,128)S(1)}, f32[4,3,512,512]{2,3,1,0:T(8,128)S(1)}) fusion(f32[4,3,512,512]{2,3,1,0:T(8,128)} %copy-done, f32[4,3,512]{2,1,0:T(4,128)S(1)} %log_add_fusion, bf16[4,512,1,3,64]{1,0,4,3,2:T(4,128)(2,1)} %copy-done.11, bf16[4,512,3,64]{1,0,3,2:T(4,128)(2,1)} %reshape.218), kind=kOutput, calls=%fused_computation.1 | convolution fusion | flops 412084224 | bytes 26787840 | tf_op jit(solution)/shard_map/bqhd,bkhd->bhqk/dot_general | solution.py:132
  526.0 6.9 multiply_convert_fusion
  532.9 2.6 copy-done.1
  536.6 1.5 copy.149
  538.1 3.2 stack.101
  541.3 5.1 fusion.21
  546.3 1.5 copy.151
  547.8 2.8 stack.102
  550.6 2.1 constant_dynamic-update-slice_fusion.2
  552.8 5.6 convolution_bitcast_fusion
  558.4 7.7 %fusion.17 = bf16[4,512,3,64]{1,3,2,0:T(8,128)(2,1)} fusion(f32[4,3,512,512]{2,3,1,0:T(8,128)} %copy-done, f32[4,3,512]{2,1,0:T(4,128)S(1)} %log_add_fusion, bf16[4,512,3,64]{1,0,3,2:T(4,128)(2,1)} %reshape.218), kind=kOutput, calls=%fused_computation.53 | convolution fusion | flops 409337856 | bytes 14180352 | tf_op jit(solution)/shard_map/bhqk,bqhd->bkhd/dot_general | solution.py:133
  566.2 2.1 constant_dynamic-update-slice_fusion.1
  568.3 2.6 copy.154
  570.9 2.8 stack.103
  573.7 2.1 constant_dynamic-update-slice_fusion
  575.8 5.8 fusion.75
  581.7 2.8 copy.179
  585.8 6.2 bitcast_convert_fusion
  595.1 1.2 dynamic-slice
  601.6 14.3 %all-reduce = f32[2,3,64]{2,1,0:T(4,128)S(1)} all-reduce(f32[2,3,64]{2,1,0:T(4,128)S(1)} %reshape.220), channel_id=10, replica_groups=mesh['dp'=8,'tensor'=4] {'dp'}, use_global_device_ids=true, to_apply=%region_17.18.clone | all-reduce | flops 384 | bytes 3072
  623.8 19.7 %reduce-scatter.20.cloned.1.call-done = f32[96,576]{1,0:T(8,128)} async-done(((f32[768,576]{1,0:T(8,128)}), f32[96,576]{1,0:T(8,128)}) %reduce-scatter.20.cloned.1.call-update) | async-done | bytes 221200
  644.8 67.8 %all-reduce.12.cloned.1.call-done = bf16[2048,768]{1,0:T(8,128)(2,1)} async-done(((bf16[2048,768]{1,0:T(8,128)(2,1)}), bf16[2048,768]{1,0:T(8,128)(2,1)}) %all-reduce.12.cloned.1.call-update) | async-done | bytes 3145744 | tf_op jit(solution)/shard_map/psum | solution.py:152
  712.5 5.4 add_reduce_fusion
  721.0 31.0 %reduce-scatter.26.cloned.1.call-done = f32[96,6]{1,0:T(8,128)} async-done(((f32[768,6]{1,0:T(8,128)}), f32[96,6]{1,0:T(8,128)}) %reduce-scatter.26.cloned.1.call-update) | async-done | bytes 2320
  (180 shorter events, 36.6 us)
Async XLA Ops:
  8.0 49.9 %copy-start.6 = (bf16[4,512,768]{2,1,0:T(8,128)(2,1)S(1)}, bf16[4,512,768]{2,1,0:T(8,128)(2,1)}, u32[]{:S(2)}) copy-start(bf16[4,512,768]{2,1,0:T(8,128)(2,1)} %param.11) | copy-start | bytes 9437188
  8.0 200.9 %all-reduce.6.cloned.1.call-start = ((), (), s32[]{:S(2)}) async-start(), calls=%async_computation.6 | async-start | bytes 6291456 | tf_op jit(solution)/shard_map/psum | solution.py:104
  71.5 4.4 copy-start.9
  71.5 4.4 copy-start.12
  71.5 6.3 copy-start.11
  76.0 4.7 copy-start
  76.0 4.7 copy-start.16
  77.8 5.3 copy-start.18
  83.9 0.9 copy-start.8
  87.5 128.3 %all-gather.10.cloned.1.call-start = ((), (), s32[]{:S(2)}) async-start(), calls=%async_computation.12 | async-start | bytes 1327104 | tf_op jit(solution)/shard_map/all_gather | solution.py:70
  89.2 134.1 %all-gather.12.cloned.1.call-start = ((), (), s32[]{:S(2)}) async-start(), calls=%async_computation.13 | async-start | bytes 1327104 | tf_op jit(solution)/shard_map/all_gather | solution.py:72
  90.9 258.8 %all-reduce.8.cloned.1.call-start = ((), (), s32[]{:S(2)}) async-start(), calls=%async_computation.7 | async-start | bytes 6291456 | tf_op jit(solution)/shard_map/psum | solution.py:111
  127.3 222.4 %copy-start.22 = (f32[768]{0:T(1024)}, f32[768]{0:T(1024)S(1)}, u32[]{:S(2)}) copy-start(f32[768]{0:T(1024)S(1)} %get-tuple-element.111) | copy-start | bytes 9220
  127.3 222.4 %copy-start.24 = (f32[768]{0:T(1024)}, f32[768]{0:T(1024)S(1)}, u32[]{:S(2)}) copy-start(f32[768]{0:T(1024)S(1)} %get-tuple-element.110) | copy-start | bytes 9220
  208.9 3.2 copy-start.7
  215.8 7.5 copy-start.20
  223.3 6.2 copy-start.36
  229.5 266.2 %all-reduce.10.cloned.1.call-start = ((), (), s32[]{:S(2)}) async-start(), calls=%async_computation.8 | async-start | bytes 6291456 | tf_op jit(solution)/shard_map/psum | solution.py:121
  354.5 1.9 copy-start.4
  356.4 7.4 slice-start
  359.4 4.3 copy-start.34
  359.4 4.3 slice-start.1
  363.8 6.0 copy-start.2
  363.8 7.7 %copy-start.33 = (bf16[1,768,768]{2,1,0:T(8,128)(2,1)S(1)}, bf16[1,768,768]{2,1,0:T(8,128)(2,1)}, u32[]{:S(2)}) copy-start(bf16[1,768,768]{2,1,0:T(8,128)(2,1)} %all-gather.10.cloned.1.call-done) | copy-start | bytes 3538948
  369.7 1.8 copy-start.35
  375.5 222.1 %reduce-scatter.24.cloned.1.call-start = ((), (), s32[]{:S(2)}) async-start(), calls=%async_computation.16 | async-start | bytes 73728
  376.3 8.1 %copy-start.17 = (f32[4,3,512]{2,1,0:T(4,128)S(1)}, f32[4,3,512]{2,1,0:T(4,128)}, u32[]{:S(2)}) copy-start(f32[4,3,512]{2,1,0:T(4,128)} %copy-done.16) | copy-start | bytes 73732
  376.4 8.1 %copy-start.19 = (f32[4,3,512]{2,1,0:T(4,128)S(1)}, f32[4,3,512]{2,1,0:T(4,128)}, u32[]{:S(2)}) copy-start(f32[4,3,512]{2,1,0:T(4,128)} %copy-done.18) | copy-start | bytes 73732
  376.4 241.5 %reduce-scatter.18.cloned.1.call-start = ((), (), s32[]{:S(2)}) async-start(), calls=%async_computation.11 | async-start | bytes 2654208 | tf_op jit(solution)/shard_map/reduce_scatter | solution.py:161
  384.4 235.6 %reduce-scatter.16.cloned.1.call-start = ((), (), s32[]{:S(2)}) async-start(), calls=%async_computation.10 | async-start | bytes 2654208 | tf_op jit(solution)/shard_map/reduce_scatter | solution.py:159
  384.5 111.2 %copy-start.23 = (f32[768]{0:T(1024)S(1)}, f32[768]{0:T(1024)}, u32[]{:S(2)}) copy-start(f32[768]{0:T(1024)} %copy-done.22) | copy-start | bytes 9220
  392.5 111.2 %copy-start.21 = (f32[2048]{0:T(1024)S(1)}, f32[2048]{0:T(1024)}, u32[]{:S(2)}) copy-start(f32[2048]{0:T(1024)} %copy-done.20) | copy-start | bytes 24580
  392.6 229.5 %reduce-scatter.22.cloned.1.call-start = ((), (), s32[]{:S(2)}) async-start(), calls=%async_computation.15 | async-start | bytes 884736
  495.7 8.0 %copy-start.5 = (bf16[2048,768]{1,0:T(8,128)(2,1)S(1)}, bf16[2048,768]{1,0:T(8,128)(2,1)}, u32[]{:S(2)}) copy-start(bf16[2048,768]{1,0:T(8,128)(2,1)} %all-reduce.10.cloned.1.call-done) | copy-start | bytes 9437188
  509.8 2.6 copy-start.3
  526.0 9.5 %copy-start.13 = (bf16[4,512,1,3,64]{1,0,4,3,2:T(4,128)(2,1)S(1)}, bf16[4,512,1,3,64]{1,0,4,3,2:T(4,128)(2,1)}, u32[]{:S(2)}) copy-start(bf16[4,512,1,3,64]{1,0,4,3,2:T(4,128)(2,1)} %copy-done.12) | copy-start | bytes 2359300
  532.9 2.6 copy-start.1
  566.2 77.4 %reduce-scatter.20.cloned.1.call-start = ((), (), s32[]{:S(2)}) async-start(), calls=%async_computation.14 | async-start | bytes 2211840
  584.5 128.0 %all-reduce.12.cloned.1.call-start = ((), (), s32[]{:S(2)}) async-start(), calls=%async_computation.9 | async-start | bytes 6291456 | tf_op jit(solution)/shard_map/psum | solution.py:152
  585.8 8.3 %copy-start.27 = (f32[768]{0:T(1024)S(1)}, f32[768]{0:T(1024)}, u32[]{:S(2)}) copy-start(f32[768]{0:T(1024)} %convert_reduce_fusion) | copy-start | bytes 9220
  585.8 11.7 %copy-start.25 = (f32[768]{0:T(1024)S(1)}, f32[768]{0:T(1024)}, u32[]{:S(2)}) copy-start(f32[768]{0:T(1024)} %get-tuple-element.104) | copy-start | bytes 9220
  585.8 15.2 %copy-start.26 = (f32[768]{0:T(1024)S(1)}, f32[768]{0:T(1024)}, u32[]{:S(2)}) copy-start(f32[768]{0:T(1024)} %get-tuple-element.107) | copy-start | bytes 9220
  592.1 9.0 %copy-start.10 = (bf16[2048,3,192]{0,2,1:T(8,128)(2,1)S(1)}, bf16[2048,3,192]{0,2,1:T(8,128)(2,1)}, u32[]{:S(2)}) copy-start(bf16[2048,3,192]{0,2,1:T(8,128)(2,1)} %constant_dynamic-update-slice_fusion) | copy-start | bytes 7077892
  592.1 31.0 %copy-start.15 = (f32[3,192,96]{2,1,0:T(8,128)S(1)}, f32[3,192,96]{2,1,0:T(8,128)}, u32[]{:S(2)}) copy-start(f32[3,192,96]{2,1,0:T(8,128)} %param.17) | copy-start | bytes 663556
  592.1 159.8 %reduce-scatter.26.cloned.1.call-start = ((), (), s32[]{:S(2)}) async-start(), calls=%async_computation.17 | async-start | bytes 442368
  598.4 119.6 %copy-start.28 = (f32[6,16]{1,0:T(8,128)}, f32[6,16]{1,0:T(8,128)S(1)}, u32[]{:S(2)}) copy-start(f32[6,16]{1,0:T(8,128)S(1)} %copy.176) | copy-start | bytes 1156
  616.6 101.3 %copy-start.30 = (f32[2,3,8]{2,0,1:T(2,128)}, f32[2,3,8]{2,0,1:T(2,128)S(1)}, u32[]{:S(2)}) copy-start(f32[2,3,8]{2,0,1:T(2,128)S(1)} %get-tuple-element.115) | copy-start | bytes 580
  623.1 94.8 %copy-start.14 = (f32[192,96]{1,0:T(8,128)}, f32[192,96]{1,0:T(8,128)S(1)}, u32[]{:S(2)}) copy-start(f32[192,96]{1,0:T(8,128)S(1)} %copy.174) | copy-start | bytes 221188
  644.7 73.2 %copy-start.31 = (f32[1,768]{1,0:T(1,128)S(1)}, f32[1,768]{1,0:T(1,128)}, u32[]{:S(2)}) copy-start(f32[1,768]{1,0:T(1,128)} %reshape.225) | copy-start | bytes 9220
  644.7 108.1 %copy-start.32 = (f32[3,6,96]{2,1,0:T(8,128)S(1)}, f32[3,6,96]{2,1,0:T(8,128)}, u32[]{:S(2)}) copy-start(f32[3,6,96]{2,1,0:T(8,128)} %param.21) | copy-start | bytes 20740
  752.8 0.6 copy-start.29
Sparse Core Ops, SparseCore 0:
  87.6 121.2 all-reduce.5
  229.6 120.0 all-reduce.7
  375.6 120.0 all-reduce.9
  592.2 120.2 all-reduce.11
Sparse Core Ops, SparseCore 1:
  90.4 25.2 all-gather.9
  118.0 23.8 all-gather.11
  379.6 32.5 reduce-scatter.23
  416.1 42.2 reduce-scatter.17
  462.2 42.2 reduce-scatter.15
  566.2 33.9 reduce-scatter.21
  603.5 40.0 reduce-scatter.19
  719.0 32.9 reduce-scatter.25
where the time goes:
time: 772 us; the launch traced here: 761 us
  waiting for transfers between devices  423 us (55%)
  matrix products  94.3 us (12%)
  local copies, waits for them, and re-layouts  90.2 us (12%)
  blocking collectives  71.4 us (9%)
  other arithmetic  63 us (8%)
  between operations  17.6 us (2%)
    psum x1, waiting for transfers between devices, body(): ffn = lax.psum(ffn_part.astype(jnp.bfloat16), 'tensor').astype(jnp.float32)  120 us
    psum x1, waiting for transfers between devices, body(): lax.psum(feed_part.astype(jnp.bfloat16), 'tensor').astype(jnp.float32)  103 us
    psum x1, waiting for transfers between devices, body(): lax.psum(attn_part.astype(jnp.bfloat16), 'tensor').astype(jnp.float32)  81.6 us
    psum x1, waiting for transfers between devices, body(): lax.psum(input_part.astype(jnp.bfloat16), 'tensor').astype(jnp.float32)  67.8 us
    unnamed x16, waiting for transfers between devices  50.9 us
    unnamed x98, local copies, waits for them, and re-layouts  29.5 us
    reduce_sum x4, other arithmetic, layer_norm(): center = value - jnp.mean(value, axis=-1, keepdims=True)  18.3 us
    dot_general x2, matrix products, contract_rows(): lax.dot_general(left, right, (((0,), (0,)), ((), ())), preferred_element_...  16 us
  transfers between devices with their start and end apart: 12, of which 6 were waited for; matrix products, arithmetic and copies ran while one was open for 21% of the time, Pallas kernels for 0%

commit v1 on v0

--- a/solution.py
+++ b/solution.py
@@ -10,6 +10,19 @@
 beta_second = 0.999
 warm_steps = 10000.0
 total_steps = 200000.0
+
+
+def gather_around(x, axis, dim):
+    length, position, rows = (lax.axis_size(axis), lax.axis_index(axis), x.shape[dim])
+    right = [(i, (i + 1) % length) for i in range(length)]
+    out = jnp.zeros((*x.shape[:dim], length * rows, *x.shape[dim + 1 :]), x.dtype)
+    block = x
+    for step in range(length):
+        owner = (position - step) % length
+        out = lax.dynamic_update_slice_in_dim(out, block, owner * rows, axis=dim)
+        if step < length - 1:
+            block = lax.ppermute(block, axis, right)
+    return out
 
 
 def layer_norm(value, gain, shift):
@@ -64,7 +77,7 @@
     bf = jnp.bfloat16
     fl = jnp.float32
     w_qkv, b_qv, w_out, w_up, b_up, w_down, vectors = (
-        lax.all_gather(qkv_state[0].astype(bf), "dp", axis=0, tiled=True),
+        gather_around(qkv_state[0].astype(bf), "dp", 0),
         lax.all_gather(qv_bias_state[0].astype(bf), "dp", axis=2, tiled=True),
         lax.all_gather(out_state[0].astype(bf), "dp", axis=1, tiled=True),
         lax.all_gather(up_state[0].astype(bf), "dp", axis=0, tiled=True),

time: 772 us -> 809 us (1.048)
  local copies, waits for them, and re-layouts: 90.2 us -> 121 us
  waiting for transfers between devices: 423 us -> 451 us
  blocking collectives: 71.4 us -> 55.5 us
    ppermute x0 -> x7, waiting for transfers between devices: none -> 27.1 us  [gather_around(): block = lax.ppermute(block, axis, right)]
    dynamic_update_slice x0 -> x8, local copies, waits for them, and re-layouts: none -> 18.9 us  [gather_around(): out = lax.dynamic_update_slice_in_dim(out, block, owner * rows, axis=dim)]
    all_gather x1 -> x0, blocking collectives: 15.8 us -> none  [body(): lax.all_gather(qkv_state[0].astype(bf), 'dp', axis=0, tiled=True)]
    ppermute x0 -> x7, local copies, waits for them, and re-layouts: none -> 12 us  [gather_around(): block = lax.ppermute(block, axis, right)]
    unnamed x98 -> x106, local copies, waits for them, and re-layouts: 29.5 us -> 31.4 us
  transfers between devices with their start and end apart: 12 -> 19, of which waited for: 6 -> 11; matrix products, arithmetic and copies ran while one was open for 21% -> 24% of each run, Pallas kernels for 0% -> 0%
where the time goes in v1:
time: 809 us; the launch traced here: 805 us
  waiting for transfers between devices  451 us (56%)
  local copies, waits for them, and re-layouts  121 us (15%)
  matrix products  96.3 us (12%)
  other arithmetic  61.6 us (8%)
  blocking collectives  55.5 us (7%)
  between operations  17.8 us (2%)
    psum x1, waiting for transfers between devices, body(): ffn = lax.psum(ffn_part.astype(jnp.bfloat16), 'tensor').astype(jnp.float32)  120 us
    psum x1, waiting for transfers between devices, body(): lax.psum(feed_part.astype(jnp.bfloat16), 'tensor').astype(jnp.float32)  103 us
    psum x1, waiting for transfers between devices, body(): lax.psum(attn_part.astype(jnp.bfloat16), 'tensor').astype(jnp.float32)  82.1 us
    psum x1, waiting for transfers between devices, body(): lax.psum(input_part.astype(jnp.bfloat16), 'tensor').astype(jnp.float32)  67.7 us
    unnamed x16, waiting for transfers between devices  50.9 us
    unnamed x106, local copies, waits for them, and re-layouts  31.4 us
    ppermute x7, waiting for transfers between devices, gather_around(): block = lax.ppermute(block, axis, right)  27.1 us
    dynamic_update_slice x8, local copies, waits for them, and re-layouts, gather_around(): out = lax.dynamic_update_slice_in_dim(out, block, owner * rows, axis=dim)  18.9 us
  transfers between devices with their start and end apart: 19, of which 11 were waited for; matrix products, arithmetic and copies ran while one was open for 24% of the time, Pallas kernels for 0%

profile of v1, /device:TPU:0, one launch (start us, length us, event | category | flops | bytes accessed | tf_op | source)
XLA Modules:
  0.0 804.8 jit_solution(4725918898749165559)
XLA Ops:
  9.8 5.7 collective-permute-done
  16.1 5.5 collective-permute-done.1
  22.2 5.5 collective-permute-done.2
  28.4 5.5 collective-permute-done.3
  33.8 2.3 broadcast_compare_fusion
  37.0 9.9 %all-gather = bf16[1,2,3,64]{2,1,0,3:T(2,128)(2,1)S(1)} all-gather(bf16[1,2,3,8]{2,1,0,3:T(2,128)(2,1)S(1)} %copy.213), channel_id=2, replica_groups=mesh['dp'=8,'tensor'=4] {'dp'}, dimensions={3}, use_global_device_ids=true | all-gather | bytes 864 | tf_op jit(solution)/shard_map/all_gather | solution.py:81
  47.6 5.0 collective-permute-done.5
  54.6 12.2 %all-gather.1 = bf16[1,192,768]{1,0,2:T(2,128)(2,1)} all-gather(bf16[1,192,96]{1,0,2:T(2,128)(2,1)S(1)} %copy.174), channel_id=3, replica_groups=mesh['dp'=8,'tensor'=4] {'dp'}, dimensions={2}, use_global_device_ids=true | all-gather | bytes 331776 | tf_op jit(solution)/shard_map/all_gather | solution.py:82
  66.8 2.4 copy.175
  73.9 2.1 dynamic_update_slice.25
  77.8 2.6 dynamic_update_slice.26
  82.1 2.6 dynamic_update_slice.27
  90.0 2.6 dynamic_update_slice.29
  94.3 2.6 dynamic_update_slice.30
  98.6 2.6 dynamic_update_slice.31
  101.2 4.6 fusion.13
  105.8 6.2 reshape.215
  112.0 2.4 fusion.70
  114.4 4.4 fusion.74
  120.7 2.8 copy-done
  123.6 2.9 fusion.23
  128.2 2.7 convolution_convert_fusion.2
  136.7 9.4 %all-gather.4 = bf16[1,6,128]{1,0,2:T(2,128)(2,1)S(1)} all-gather(bf16[1,6,16]{1,0,2:T(2,128)(2,1)} %copy.177), channel_id=6, replica_groups=mesh['dp'=8,'tensor'=4] {'dp'}, dimensions={2}, use_global_device_ids=true | all-gather | bytes 1728 | tf_op jit(solution)/shard_map/all_gather | solution.py:84
  147.4 9.8 %all-gather.2 = bf16[1,6,768]{1,0,2:T(2,128)(2,1)S(1)} all-gather(bf16[1,6,96]{1,0,2:T(2,128)(2,1)S(1)} %copy.217), channel_id=4, replica_groups=mesh['dp'=8,'tensor'=4] {'dp'}, dimensions={2}, use_global_device_ids=true | all-gather | bytes 10368 | tf_op jit(solution)/shard_map/all_gather | solution.py:86
  157.6 13.0 %slice_reduce_fusion.1 = (f32[768]{0:T(1024)S(1)}, f32[768]{0:T(1024)S(1)}, f32[768]{0:T(1024)S(1)}, f32[768]{0:T(1024)S(1)}, f32[768]{0:T(1024)S(1)}, /*index=5*/f32[768]{0:T(1024)S(1)}) fusion(f32[1,6,768]{1,0,2:T(1,128)S(1)} %convert_element_type.173), kind=kLoop, calls=%fused_computation.78 | loop fusion | bytes 36864 | tf_op jit(solution)/shard_map/slice | solution.py:125
  170.6 82.1 %all-reduce.6.cloned.1.call-done = bf16[2048,768]{1,0:T(8,128)(2,1)} async-done(((bf16[2048,768]{1,0:T(8,128)(2,1)}), bf16[2048,768]{1,0:T(8,128)(2,1)}) %all-reduce.6.cloned.1.call-update) | async-done | bytes 3145744 | tf_op jit(solution)/shard_map/psum | solution.py:117
  252.7 3.1 fusion.11
  255.8 3.6 multiply_reduce_fusion.4
  259.5 7.4 multiply_convert_fusion.1
  266.9 6.2 convolution_convert_fusion.1
  273.2 120.2 %all-reduce.8.cloned.1.call-done = bf16[2048,768]{1,0:T(8,128)(2,1)} async-done(((bf16[2048,768]{1,0:T(8,128)(2,1)}), bf16[2048,768]{1,0:T(8,128)(2,1)}) %all-reduce.8.cloned.1.call-update) | async-done | bytes 3145744 | tf_op jit(solution)/shard_map/psum | solution.py:124
  393.4 4.9 fusion.68
  400.2 3.0 fusion.7
  403.3 4.3 fusion.67
  407.6 5.9 convert_reduce_fusion.1
  415.3 4.0 convolution_convert_fusion
  420.2 8.0 fusion.61
  428.3 8.0 fusion.62
  436.4 103.1 %all-reduce.10.cloned.1.call-done = bf16[2048,768]{1,0:T(8,128)(2,1)} async-done(((bf16[2048,768]{1,0:T(8,128)(2,1)}), bf16[2048,768]{1,0:T(8,128)(2,1)}) %all-reduce.10.cloned.1.call-update) | async-done | bytes 3145744 | tf_op jit(solution)/shard_map/psum | solution.py:134
  539.6 8.2 %multiply_reduce_fusion.1 = (f32[768]{0:T(1024)}, f32[2048]{0:T(1024)S(1)}, f32[768]{0:T(1024)}, f32[768]{0:T(1024)}) fusion(f32[2048,768]{1,0:T(8,128)} %get-tuple-element.123, f32[2048]{0:T(1024)S(1)} %fusion.50, bf16[2048,768]{1,0:T(8,128)(2,1)} %all-reduce.10.cloned.1.call-done, f32[2048,768]{1,0:T(8,128)} %copy-done.2, ...), kind=kLoop, calls=%fused_computation.19 | loop fusion | flops 17297152 | bytes 15765504 | tf_op jit(solution)/shard_map/transpose(jvp())/reduce_sum | solution.py:31
  547.8 6.1 fusion.66
  553.9 2.6 copy-done.3
  556.4 2.2 convolution_convert_fusion.3
  558.6 3.0 reshape.218
  561.6 8.3 %multiply_reduce_fusion = (f32[4,3,512]{2,1,0:T(4,128)S(1)}, f32[4,3,512,512]{2,3,1,0:T(8,128)S(1)}) fusion(f32[4,3,512,512]{2,3,1,0:T(8,128)} %copy-done, f32[4,3,512]{2,1,0:T(4,128)S(1)} %log_add_fusion, bf16[4,512,1,3,64]{1,0,4,3,2:T(4,128)(2,1)} %copy-done.11, bf16[4,512,3,64]{1,0,3,2:T(4,128)(2,1)} %reshape.218), kind=kOutput, calls=%fused_computation.1 | convolution fusion | flops 412084224 | bytes 26787840 | tf_op jit(solution)/shard_map/bqhd,bkhd->bhqk/dot_general | solution.py:145
  570.0 6.9 multiply_convert_fusion
  576.9 2.6 copy-done.1
  582.1 3.2 stack.101
  585.3 5.1 fusion.22
  591.8 2.8 stack.102
  594.6 2.1 constant_dynamic-update-slice_fusion.2
  596.7 5.6 convolution_bitcast_fusion
  602.3 7.7 fusion.18
  612.3 2.6 copy.186
  614.9 2.8 stack.103
  617.7 2.1 constant_dynamic-update-slice_fusion
  619.8 5.8 fusion.75
  625.7 2.8 copy.211
  629.8 6.2 bitcast_convert_fusion
  645.6 14.3 %all-reduce = f32[2,3,64]{2,1,0:T(4,128)S(1)} all-reduce(f32[2,3,64]{2,1,0:T(4,128)S(1)} %reshape.220), channel_id=9, replica_groups=mesh['dp'=8,'tensor'=4] {'dp'}, use_global_device_ids=true, to_apply=%region_17.18.clone | all-reduce | flops 384 | bytes 3072
  667.8 19.7 %reduce-scatter.20.cloned.1.call-done = f32[96,576]{1,0:T(8,128)} async-done(((f32[768,576]{1,0:T(8,128)}), f32[96,576]{1,0:T(8,128)}) %reduce-scatter.20.cloned.1.call-update) | async-done | bytes 221200
  688.8 67.7 %all-reduce.12.cloned.1.call-done = bf16[2048,768]{1,0:T(8,128)(2,1)} async-done(((bf16[2048,768]{1,0:T(8,128)(2,1)}), bf16[2048,768]{1,0:T(8,128)(2,1)}) %all-reduce.12.cloned.1.call-update) | async-done | bytes 3145744 | tf_op jit(solution)/shard_map/psum | solution.py:165
  756.5 5.4 add_reduce_fusion
  765.0 31.0 %reduce-scatter.26.cloned.1.call-done = f32[96,6]{1,0:T(8,128)} async-done(((f32[768,6]{1,0:T(8,128)}), f32[96,6]{1,0:T(8,128)}) %reduce-scatter.26.cloned.1.call-update) | async-done | bytes 2320
  (215 shorter events, 69.0 us)
Async XLA Ops:
  8.0 93.2 %copy-start.6 = (bf16[4,512,768]{2,1,0:T(8,128)(2,1)S(1)}, bf16[4,512,768]{2,1,0:T(8,128)(2,1)}, u32[]{:S(2)}) copy-start(bf16[4,512,768]{2,1,0:T(8,128)(2,1)} %param.11) | copy-start | bytes 9437188
  8.0 244.6 %all-reduce.6.cloned.1.call-start = ((), (), s32[]{:S(2)}) async-start(), calls=%async_computation.6 | async-start | bytes 6291456 | tf_op jit(solution)/shard_map/psum | solution.py:117
  9.2 6.2 collective-permute-start
  15.5 0.7 copy-start.16
  16.1 5.5 collective-permute-start.1
  21.6 0.7 copy-start.17
  22.2 5.5 collective-permute-start.2
  27.7 0.7 copy-start.18
  28.4 5.5 collective-permute-start.3
  33.8 20.8 %copy-start.19 = (bf16[96,3,192]{2,0,1:T(8,128)(2,1)}, bf16[96,3,192]{2,0,1:T(8,128)(2,1)S(1)}, u32[]{:S(2)}) copy-start(bf16[96,3,192]{2,0,1:T(8,128)(2,1)S(1)} %collective-permute-done.3) | copy-start | bytes 331780
  33.8 13.0 %collective-permute-start.4 = (bf16[96,3,192]{2,0,1:T(8,128)(2,1)S(1)}, bf16[96,3,192]{2,0,1:T(8,128)(2,1)}, u32[]{:S(2)}, u32[]{:S(2)}) collective-permute-start(bf16[96,3,192]{2,0,1:T(8,128)(2,1)S(1)} %collective-permute-done.3), channel_id=1, source_target_pairs={{0,4},{4,8},{8,12},{12,16},{16,20},{20,24},{24,28},{28,0},{1,5},{5... | collective-permute-start | bytes 331784 | tf_op jit(solution)/shard_map/ppermute | solution.py:24
  46.8 5.8 collective-permute-start.5
  52.6 44.3 %collective-permute-start.6 = (bf16[96,3,192]{2,0,1:T(8,128)(2,1)}, bf16[96,3,192]{2,0,1:T(8,128)(2,1)}, u32[]{:S(2)}, u32[]{:S(2)}) collective-permute-start(bf16[96,3,192]{2,0,1:T(8,128)(2,1)} %collective-permute-done.5), channel_id=1, source_target_pairs={{0,4},{4,8},{8,12},{12,16},{16,20},{20,24},{24,28},{28,0},{1,5},{5... | collective-permute-start | bytes 331784 | tf_op jit(solution)/shard_map/ppermute | solution.py:24
  114.4 4.4 copy-start.9
  114.4 4.4 copy-start.12
  114.4 6.3 copy-start.11
  118.9 4.7 copy-start
  118.9 4.7 copy-start.20
  120.7 5.9 copy-start.22
  127.4 0.9 copy-start.8
  131.0 128.5 %all-gather.9.cloned.1.call-start = ((), (), s32[]{:S(2)}) async-start(), calls=%async_computation.12 | async-start | bytes 1327104 | tf_op jit(solution)/shard_map/all_gather | solution.py:83
  132.7 134.3 %all-gather.11.cloned.1.call-start = ((), (), s32[]{:S(2)}) async-start(), calls=%async_computation.13 | async-start | bytes 1327104 | tf_op jit(solution)/shard_map/all_gather | solution.py:85
  134.4 259.0 %all-reduce.8.cloned.1.call-start = ((), (), s32[]{:S(2)}) async-start(), calls=%async_computation.7 | async-start | bytes 6291456 | tf_op jit(solution)/shard_map/psum | solution.py:124
  170.6 222.8 %copy-start.26 = (f32[768]{0:T(1024)}, f32[768]{0:T(1024)S(1)}, u32[]{:S(2)}) copy-start(f32[768]{0:T(1024)S(1)} %get-tuple-element.111) | copy-start | bytes 9220
  170.6 222.8 %copy-start.28 = (f32[768]{0:T(1024)}, f32[768]{0:T(1024)S(1)}, u32[]{:S(2)}) copy-start(f32[768]{0:T(1024)S(1)} %get-tuple-element.110) | copy-start | bytes 9220
  252.7 3.2 copy-start.7
  259.5 7.5 copy-start.24
  266.9 6.2 copy-start.40
  273.2 266.4 %all-reduce.10.cloned.1.call-start = ((), (), s32[]{:S(2)}) async-start(), calls=%async_computation.8 | async-start | bytes 6291456 | tf_op jit(solution)/shard_map/psum | solution.py:134
  398.3 1.9 copy-start.4
  400.2 7.4 slice-start
  403.3 4.3 copy-start.38
  403.3 4.3 slice-start.1
  407.6 6.0 copy-start.2
  407.6 7.7 copy-start.37
  413.6 1.7 copy-start.39
  419.3 222.2 %reduce-scatter.24.cloned.1.call-start = ((), (), s32[]{:S(2)}) async-start(), calls=%async_computation.16 | async-start | bytes 73728
  420.2 8.1 %copy-start.21 = (f32[4,3,512]{2,1,0:T(4,128)S(1)}, f32[4,3,512]{2,1,0:T(4,128)}, u32[]{:S(2)}) copy-start(f32[4,3,512]{2,1,0:T(4,128)} %copy-done.20) | copy-start | bytes 73732
  420.2 8.1 %copy-start.23 = (f32[4,3,512]{2,1,0:T(4,128)S(1)}, f32[4,3,512]{2,1,0:T(4,128)}, u32[]{:S(2)}) copy-start(f32[4,3,512]{2,1,0:T(4,128)} %copy-done.22) | copy-start | bytes 73732
  420.2 241.7 %reduce-scatter.18.cloned.1.call-start = ((), (), s32[]{:S(2)}) async-start(), calls=%async_computation.11 | async-start | bytes 2654208 | tf_op jit(solution)/shard_map/reduce_scatter | solution.py:174
  428.2 235.8 %reduce-scatter.16.cloned.1.call-start = ((), (), s32[]{:S(2)}) async-start(), calls=%async_computation.10 | async-start | bytes 2654208 | tf_op jit(solution)/shard_map/reduce_scatter | solution.py:172
  428.3 111.2 %copy-start.27 = (f32[768]{0:T(1024)S(1)}, f32[768]{0:T(1024)}, u32[]{:S(2)}) copy-start(f32[768]{0:T(1024)} %copy-done.26) | copy-start | bytes 9220
  436.4 111.4 %copy-start.25 = (f32[2048]{0:T(1024)S(1)}, f32[2048]{0:T(1024)}, u32[]{:S(2)}) copy-start(f32[2048]{0:T(1024)} %copy-done.24) | copy-start | bytes 24580
  436.4 229.7 %reduce-scatter.22.cloned.1.call-start = ((), (), s32[]{:S(2)}) async-start(), calls=%async_computation.15 | async-start | bytes 884736
  539.6 8.2 %copy-start.5 = (bf16[2048,768]{1,0:T(8,128)(2,1)S(1)}, bf16[2048,768]{1,0:T(8,128)(2,1)}, u32[]{:S(2)}) copy-start(bf16[2048,768]{1,0:T(8,128)(2,1)} %all-reduce.10.cloned.1.call-done) | copy-start | bytes 9437188
  553.8 2.6 copy-start.3
  570.0 9.5 %copy-start.13 = (bf16[4,512,1,3,64]{1,0,4,3,2:T(4,128)(2,1)S(1)}, bf16[4,512,1,3,64]{1,0,4,3,2:T(4,128)(2,1)}, u32[]{:S(2)}) copy-start(bf16[4,512,1,3,64]{1,0,4,3,2:T(4,128)(2,1)} %copy-done.12) | copy-start | bytes 2359300
  576.9 2.6 copy-start.1
  610.1 77.4 %reduce-scatter.20.cloned.1.call-start = ((), (), s32[]{:S(2)}) async-start(), calls=%async_computation.14 | async-start | bytes 2211840
  628.5 128.0 %all-reduce.12.cloned.1.call-start = ((), (), s32[]{:S(2)}) async-start(), calls=%async_computation.9 | async-start | bytes 6291456 | tf_op jit(solution)/shard_map/psum | solution.py:165
  629.8 8.3 %copy-start.31 = (f32[768]{0:T(1024)S(1)}, f32[768]{0:T(1024)}, u32[]{:S(2)}) copy-start(f32[768]{0:T(1024)} %convert_reduce_fusion) | copy-start | bytes 9220
  629.8 11.7 %copy-start.29 = (f32[768]{0:T(1024)S(1)}, f32[768]{0:T(1024)}, u32[]{:S(2)}) copy-start(f32[768]{0:T(1024)} %get-tuple-element.104) | copy-start | bytes 9220
  629.8 15.2 %copy-start.30 = (f32[768]{0:T(1024)S(1)}, f32[768]{0:T(1024)}, u32[]{:S(2)}) copy-start(f32[768]{0:T(1024)} %get-tuple-element.107) | copy-start | bytes 9220
  636.1 9.0 %copy-start.10 = (bf16[2048,3,192]{0,2,1:T(8,128)(2,1)S(1)}, bf16[2048,3,192]{0,2,1:T(8,128)(2,1)}, u32[]{:S(2)}) copy-start(bf16[2048,3,192]{0,2,1:T(8,128)(2,1)} %constant_dynamic-update-slice_fusion) | copy-start | bytes 7077892
  636.1 31.0 %copy-start.15 = (f32[3,192,96]{2,1,0:T(8,128)S(1)}, f32[3,192,96]{2,1,0:T(8,128)}, u32[]{:S(2)}) copy-start(f32[3,192,96]{2,1,0:T(8,128)} %param.17) | copy-start | bytes 663556
  636.1 159.8 %reduce-scatter.26.cloned.1.call-start = ((), (), s32[]{:S(2)}) async-start(), calls=%async_computation.17 | async-start | bytes 442368
  642.4 119.6 %copy-start.32 = (f32[6,16]{1,0:T(8,128)}, f32[6,16]{1,0:T(8,128)S(1)}, u32[]{:S(2)}) copy-start(f32[6,16]{1,0:T(8,128)S(1)} %copy.208) | copy-start | bytes 1156
  660.6 101.3 %copy-start.34 = (f32[2,3,8]{2,0,1:T(2,128)}, f32[2,3,8]{2,0,1:T(2,128)S(1)}, u32[]{:S(2)}) copy-start(f32[2,3,8]{2,0,1:T(2,128)S(1)} %get-tuple-element.115) | copy-start | bytes 580
  667.1 94.8 %copy-start.14 = (f32[192,96]{1,0:T(8,128)}, f32[192,96]{1,0:T(8,128)S(1)}, u32[]{:S(2)}) copy-start(f32[192,96]{1,0:T(8,128)S(1)} %copy.206) | copy-start | bytes 221188
  688.8 73.2 %copy-start.35 = (f32[1,768]{1,0:T(1,128)S(1)}, f32[1,768]{1,0:T(1,128)}, u32[]{:S(2)}) copy-start(f32[1,768]{1,0:T(1,128)} %reshape.225) | copy-start | bytes 9220
  688.8 108.1 %copy-start.36 = (f32[3,6,96]{2,1,0:T(8,128)S(1)}, f32[3,6,96]{2,1,0:T(8,128)}, u32[]{:S(2)}) copy-start(f32[3,6,96]{2,1,0:T(8,128)} %param.21) | copy-start | bytes 20740
  796.8 0.6 copy-start.33
Sparse Core Ops, SparseCore 0:
  131.1 121.5 all-reduce.5
  273.3 120.0 all-reduce.7
  419.5 120.0 all-reduce.9
  636.2 120.2 all-reduce.11
Sparse Core Ops, SparseCore 1:
  133.9 25.4 all-gather.8
  161.7 23.8 all-gather.10
  423.4 32.5 reduce-scatter.23
  459.9 42.2 reduce-scatter.17
  506.1 42.2 reduce-scatter.15
  610.2 33.9 reduce-scatter.21
  647.4 40.1 reduce-scatter.19
  763.0 32.9 reduce-scatter.25
